TPU v7x, 256 devices: a whole 4x4x8 slice. The times are simulated.
256 devices in a mesh: seq: 64 (over x, z, core), tp: 4 (over y).
Axes of the slice: x: 4, y: 4, z: 8, core: 2. Of those that a mesh axis runs over, the one named last changes fastest.
Arguments:
- queries: bfloat16 [65536, 2048], P('seq', 'tp'), may hold values from -6.5 to 6.5
- db_keys: bfloat16 [1024, 128, 2048], P('seq', None, 'tp'), may hold values from -6 to 6
- db_values: bfloat16 [1024, 128, 2048], P('seq', None, 'tp'), may hold values from -12 to 12
- nb_shard: int32 [1024, 2], P('seq'), may hold values from 0 to 63, all different within a row; in each aligned block of 16 rows (0 to 15, 16 to 31, ...) at most 2 rows name the same one
- nb_row: int32 [1024, 2], P('seq'), may hold values from 0 to 15
- out_weight: bfloat16 [2048, 4096], P('seq', 'tp'), may hold values from -0.125 to 0.125
Outputs:
- mixed: bfloat16 [65536, 4096], P('seq', 'tp')
Inputs may be any that keep to these rules, and one draw needn't show every extreme that they name: `nb_shard`: among the 16 blocks of one index of seq no shard is named more than 2 times, a bound that some block reaches in some such group; the 2 shards of one block differ.
All inputs are finite; a program needn't handle non-finite values.
Results may differ from a plain program's by a relative error of at most 0.024.
Values may be sent and summed in bfloat16 or wider, within the bound.
No kernel may reach another device: no remote copies, remote signals or barrier semaphores. Data moves between devices by JAX's collectives and lax.ppermute only.
A program may use at most 192 MiB of HBM per device.

v0:
```python
import jax
import jax.numpy as jnp
from jax import lax
from jax.sharding import PartitionSpec as P

HD = 128
BLOCK = 64
NBR = 2
NLEN = 128


def from_behind(shard, axis, by):
    count = lax.axis_size(axis)
    pairs = [(i, i + by) for i in range(count) if 0 <= i + by < count]
    return lax.ppermute(shard, axis, pairs)


def per_device(queries, db_keys, db_values, nb_shard, nb_row, out_weight):
    score_scale = float(HD) ** (-0.5)
    tok_rows = queries.shape[0]
    feature_cols = queries.shape[1]
    heads_here = feature_cols // HD
    blocks = tok_rows // BLOCK
    shards = lax.axis_size("seq")
    capacity = max(2, 4 * blocks // shards)
    upcoming = from_behind(queries[:BLOCK], "seq", -1)
    extended = jnp.concatenate([queries[BLOCK - 1 :], upcoming[: BLOCK - 1]], axis=0).reshape(
        blocks, BLOCK, feature_cols
    )
    owners = nb_shard.reshape(-1)
    entries = nb_row.reshape(-1)
    requests = owners.shape[0]
    positions = jnp.arange(requests, dtype=jnp.int32)
    same_owner = (owners[:, None] == owners[None, :]) & (positions[None, :] < positions[:, None])
    slot_rank = jnp.sum(same_owner.astype(jnp.int32), axis=1)
    slot_index = owners * capacity + slot_rank
    outgoing = (
        jnp.zeros((shards * capacity, BLOCK, feature_cols), jnp.bfloat16)
        .at[slot_index]
        .set(extended[positions // NBR])
    )
    outgoing = outgoing.reshape(shards, capacity, BLOCK, feature_cols)
    wanted = (
        jnp.zeros((shards * capacity,), jnp.int32)
        .at[slot_index]
        .set(entries)
        .reshape(shards, capacity)
    )
    asked_queries = lax.all_to_all(outgoing, "seq", split_axis=0, concat_axis=0, tiled=True)
    asked_rows = lax.all_to_all(wanted, "seq", split_axis=0, concat_axis=0, tiled=True)
    sources = asked_rows.shape[0]
    slots_in = asked_rows.shape[1]
    key_rows = db_keys[asked_rows].reshape(sources, slots_in, NLEN, heads_here, HD)
    value_rows = db_values[asked_rows].reshape(sources, slots_in, NLEN, heads_here, HD)
    query_heads = asked_queries.reshape(sources, slots_in, BLOCK, heads_here, HD)
    scores = (
        jnp.einsum("scqhd,sckhd->schqk", query_heads, key_rows, preferred_element_type=jnp.float32)
        * score_scale
    )
    row_max = jnp.max(scores, axis=-1, keepdims=True)
    log_total = row_max[..., 0] + jnp.log(jnp.sum(jnp.exp(scores - row_max), axis=-1))
    weights = jnp.exp(scores - log_total[..., None]).astype(jnp.bfloat16)
    partial_value = jnp.einsum(
        "schqk,sckhd->scqhd", weights, value_rows, preferred_element_type=jnp.float32
    )
    partial_value = partial_value.astype(jnp.bfloat16).reshape(
        sources, slots_in, BLOCK, feature_cols
    )
    partials = lax.all_to_all(partial_value, "seq", split_axis=0, concat_axis=0, tiled=True)
    log_totals = lax.all_to_all(
        log_total.astype(jnp.bfloat16), "seq", split_axis=0, concat_axis=0, tiled=True
    ).astype(log_total.dtype)
    partials = partials.reshape(shards * capacity, BLOCK, feature_cols)[slot_index]
    partials = partials.reshape(blocks, NBR, BLOCK, heads_here, HD)
    log_totals = log_totals.reshape(shards * capacity, heads_here, BLOCK)[slot_index]
    log_totals = log_totals.reshape(blocks, NBR, heads_here, BLOCK)
    best_log = jnp.max(log_totals, axis=1, keepdims=True)
    merged_log = best_log + jnp.log(jnp.sum(jnp.exp(log_totals - best_log), axis=1, keepdims=True))
    share = jnp.transpose(jnp.exp(log_totals - merged_log), (0, 1, 3, 2))[..., None]
    attended = jnp.sum(share * partials.astype(jnp.float32), axis=1).astype(jnp.bfloat16)
    attended = attended.reshape(blocks * BLOCK, feature_cols)
    tail_rows = from_behind(attended[-BLOCK:], "seq", 1)
    placed = jnp.concatenate([tail_rows[1:], attended[: tok_rows - (BLOCK - 1)]], axis=0)
    rows_all = lax.all_gather(out_weight, "seq", axis=0, tiled=True)
    own_rows = lax.all_to_all(rows_all, "tp", split_axis=0, concat_axis=1, tiled=True)
    terms = jnp.dot(placed, own_rows, preferred_element_type=jnp.float32)
    mixed = lax.psum_scatter(terms.astype(jnp.bfloat16), "tp", scatter_dimension=1, tiled=True)
    return mixed


def solution(mesh):
    placed = (
        P("seq", "tp"),
        P("seq", None, "tp"),
        P("seq", None, "tp"),
        P("seq", None),
        P("seq", None),
        P("seq", "tp"),
    )
    return jax.shard_map(
        per_device, mesh=mesh, in_specs=placed, out_specs=P("seq", "tp"), check_vma=False
    )
```

profile of v0, /device:TPU:1, one launch (start us, length us, event | category | flops | bytes accessed | tf_op | source)
XLA Modules:
  0.0 665.3 jit_solution(10887075580433408227)
XLA Ops:
  6.5 0.0 copy-start
  6.5 0.8 broadcast_multiply_fusion
  7.4 0.8 copy.49
  8.1 0.1 copy.48
  8.2 0.1 mul.32
  8.3 0.1 eq.15
  8.4 0.2 convert_reduce_fusion
  8.6 0.8 copy.50
  9.3 0.1 reshape.232
  9.4 0.7 scatter_custom_fusion.1
  10.1 0.7 all_to_all.32
  10.9 13.0 %all-to-all-start.1 = ((s32[64,1,2]{2,1,0:T(1,128)}), s32[64,1,2]{2,1,0:T(1,128)S(1)}, u32[]{:S(2)}, u32[]{:S(2)}) async-start(s32[64,1,2]{2,1,0:T(1,128)} %bitcast.5), calls=%async_computation.1 | async-start | bytes 65536 | tf_op jit(solution)/shard_map/all_to_all | solution.py:50
  23.8 0.8 slice.22
  24.7 2.4 collective-permute-start
  27.1 1.4 slice.21
  28.5 2.0 collective-permute-done
  30.6 0.1 pad_maximum_fusion
  30.6 2.0 gather_fusion
  32.6 4.2 broadcast_in_dim.4
  36.9 6.3 scatter_fusion
  43.1 0.0 all-to-all-done.1
  43.1 10.0 %all-to-all-start = ((bf16[64,2,64,512]{3,2,1,0:T(8,128)(2,1)}), bf16[64,2,64,512]{3,2,1,0:T(8,128)(2,1)}, u32[]{:S(2)}, u32[]{:S(2)}) async-start(bf16[64,2,64,512]{3,2,1,0:T(8,128)(2,1)} %bitcast.66), calls=%async_computation | async-start | bytes 16777216 | tf_op jit(solution)/shard_map/all_to_all | solution.py:49
  53.1 0.1 copy.52
  53.2 0.1 copy.53
  53.3 0.1 reshape.190
  53.5 0.0 copy-done
  53.5 7.8 %gather_fusion.1 = bf16[128,128,512]{2,1,0:T(8,128)(2,1)} fusion(bf16[16,128,512]{2,1,0:T(8,128)(2,1)S(1)} %copy-done, s32[1024]{0:T(1024)S(1)} %pad_clamp_fusion.1), kind=kCustom, calls=%fused_computation.1 | custom fusion | bytes 33554944 | tf_op jit(solution)/shard_map/gather | solution.py:53
  61.3 23.9 %reshape.170 = bf16[64,2,128,4,128]{4,3,2,1,0:T(4,128)(2,1)} reshape(bf16[128,128,512]{2,1,0:T(8,128)(2,1)} %gather_fusion.1) | data formatting | bytes 33554432 | tf_op jit(solution)/shard_map/reshape | solution.py:53
  85.2 0.0 copy-done.2
  85.2 7.9 %gather_fusion.3 = bf16[128,128,512]{2,1,0:T(8,128)(2,1)} fusion(bf16[16,128,512]{2,1,0:T(8,128)(2,1)S(1)} %copy-done.2, s32[1024]{0:T(1024)S(1)} %pad_clamp_fusion.1), kind=kCustom, calls=%fused_computation.3 | custom fusion | bytes 33554944 | tf_op jit(solution)/shard_map/gather | solution.py:54
  93.0 23.7 %reshape.174 = bf16[64,2,128,4,128]{4,3,2,1,0:T(4,128)(2,1)} reshape(bf16[128,128,512]{2,1,0:T(8,128)(2,1)} %gather_fusion.3) | data formatting | bytes 33554432 | tf_op jit(solution)/shard_map/reshape | solution.py:54
  116.7 122.2 %all-to-all-done = bf16[64,2,64,512]{3,2,1,0:T(8,128)(2,1)} async-done(((bf16[64,2,64,512]{3,2,1,0:T(8,128)(2,1)}), bf16[64,2,64,512]{3,2,1,0:T(8,128)(2,1)}, u32[]{:S(2)}, u32[]{:S(2)}) %all-to-all-start) | async-done | bytes 8388640 | tf_op jit(solution)/shard_map/all_to_all | solution.py:49
  238.9 19.9 %multiply_reduce_fusion = (f32[64,2,4,64]{3,2,1,0:T(4,128)S(1)}, f32[64,2,4,64,128]{4,3,2,1,0:T(8,128)}) fusion(bf16[64,2,128,4,128]{4,3,2,1,0:T(4,128)(2,1)} %reshape.170, bf16[64,2,64,512]{3,2,1,0:T(8,128)(2,1)} %all-to-all-done), kind=kOutput, calls=%fused_computation.13 | convolution fusion | flops 1082097664 | bytes 42074112 | tf_op jit(solution)/shard_map/scqhd,sckhd->schqk/dot_general | solution.py:57
  258.8 12.6 %exponential_reduce_fusion = f32[64,2,4,64]{3,2,1,0:T(4,128)S(1)} fusion(f32[64,2,4,64,128]{4,3,2,1,0:T(8,128)} %get-tuple-element.8, f32[64,2,4,64]{3,2,1,0:T(4,128)S(1)} %get-tuple-element.7), kind=kLoop, calls=%fused_computation.12 | loop fusion | flops 12550144 | bytes 17039360 | tf_op jit(solution)/shard_map/reduce_sum | solution.py:61
  271.4 0.1 fusion.24
  271.6 0.8 reshape.242
  272.4 5.9 all-to-all-start.2
  278.3 15.7 %convert_bitcast_fusion = bf16[64,2,4,8,8,128]{5,4,3,2,1,0:T(8,128)(2,1)} fusion(bf16[64,2,128,4,128]{4,3,2,1,0:T(4,128)(2,1)} %reshape.174, f32[64,2,4,64,128]{4,3,2,1,0:T(8,128)} %get-tuple-element.8, f32[64,2,4,64]{3,2,1,0:T(4,128)S(1)} %get-tuple-element.6), kind=kOutput, calls=%fused_computation.17 | convolution fusion | flops 1090519040 | bytes 42074112 | tf_op jit(solution)/shard_map/schqk,sckhd->scqhd/dot_general | solution.py:63
  294.0 8.4 %copy.81 = bf16[64,2,4,8,8,128]{5,4,2,3,1,0:T(8,128)(2,1)} copy(bf16[64,2,4,8,8,128]{5,4,3,2,1,0:T(8,128)(2,1)} %convert_bitcast_fusion) | data formatting | bytes 16777216 | tf_op jit(solution)/shard_map/reshape | solution.py:66
  302.4 0.0 all-to-all-done.2
  302.4 10.5 %all-to-all-start.3 = ((bf16[64,2,64,512]{3,2,1,0:T(8,128)(2,1)}), bf16[64,2,64,512]{3,2,1,0:T(8,128)(2,1)}, u32[]{:S(2)}, u32[]{:S(2)}) async-start(bf16[64,2,64,512]{3,2,1,0:T(8,128)(2,1)} %bitcast.67), calls=%async_computation.3 | async-start | bytes 16777216 | tf_op jit(solution)/shard_map/all_to_all | solution.py:69
  312.9 0.0 all-gather.2.cloned.1.call-start
  313.0 0.7 all-gather.2.cloned.1.call-update
  313.6 106.5 %all-gather.2.cloned.1.call-done = bf16[2048,1024]{1,0:T(8,128)(2,1)} async-done(((bf16[32,1024]{1,0:T(8,128)(2,1)}), bf16[2048,1024]{1,0:T(8,128)(2,1)}) %all-gather.2.cloned.1.call-update) | async-done | bytes 4194320 | tf_op jit(solution)/shard_map/all_gather | solution.py:84
  420.2 90.8 %all-to-all-done.3 = bf16[64,2,64,512]{3,2,1,0:T(8,128)(2,1)} async-done(((bf16[64,2,64,512]{3,2,1,0:T(8,128)(2,1)}), bf16[64,2,64,512]{3,2,1,0:T(8,128)(2,1)}, u32[]{:S(2)}, u32[]{:S(2)}) %all-to-all-start.3) | async-done | bytes 8388640 | tf_op jit(solution)/shard_map/all_to_all | solution.py:69
  511.0 4.9 all-to-all-start.4
  515.9 0.0 reduce-scatter.2.cloned.1.call-start
  516.0 0.1 reshape.243
  516.2 0.6 gather_fusion.2
  516.9 0.4 copy.56
  517.3 4.1 gather_fusion.4
  521.4 3.1 reshape.179
  524.4 5.0 multiply_reduce_fusion.1
  529.5 1.9 collective-permute-start.1
  531.4 33.8 %all-to-all-done.4 = bf16[4,512,1024]{2,1,0:T(8,128)(2,1)} async-done(((bf16[4,512,1024]{2,1,0:T(8,128)(2,1)}), bf16[4,512,1024]{2,1,0:T(8,128)(2,1)}, u32[]{:S(2)}, u32[]{:S(2)}) %all-to-all-start.4) | async-done | bytes 4194336 | tf_op jit(solution)/shard_map/all_to_all | solution.py:85
  565.3 6.2 copy.59
  571.5 0.2 copy.82
  571.7 0.1 slice.41
  571.7 0.0 collective-permute-done.1
  571.8 0.0 copy-start.1
  571.8 9.2 %convolution_convert_fusion = bf16[1024,4096]{1,0:T(8,128)(2,1)} fusion(bf16[512,4096]{0,1:T(8,128)(2,1)} %bitcast.71, bf16[961,512]{1,0:T(8,128)(2,1)S(1)} %slice.41, bf16[63,512]{1,0:T(8,128)(2,1)S(1)} %slice.40), kind=kOutput, calls=%fused_computation.20 | convolution fusion | flops 4301258752 | bytes 13631488 | tf_op jit(solution)/shard_map/dot_general | solution.py:86
  581.0 0.0 reduce-scatter.2.cloned.1.call-update
  581.0 77.5 %reduce-scatter.2.cloned.1.call-done = bf16[1024,1024]{1,0:T(8,128)(2,1)} async-done(((bf16[1024,4096]{1,0:T(8,128)(2,1)}), bf16[1024,1024]{1,0:T(8,128)(2,1)}) %reduce-scatter.2.cloned.1.call-update) | async-done | bytes 2097168 | tf_op jit(solution)/shard_map/reduce_scatter | solution.py:87
  658.5 0.0 copy-done.1
  (15 shorter events, 0.2 us)
Async XLA Ops:
  6.5 46.9 %copy-start = (bf16[16,128,512]{2,1,0:T(8,128)(2,1)S(1)}, bf16[16,128,512]{2,1,0:T(8,128)(2,1)}, u32[]{:S(2)}) copy-start(bf16[16,128,512]{2,1,0:T(8,128)(2,1)} %param.7) | copy-start | bytes 6291460
  10.9 32.3 %all-to-all-start.1 = ((s32[64,1,2]{2,1,0:T(1,128)}), s32[64,1,2]{2,1,0:T(1,128)S(1)}, u32[]{:S(2)}, u32[]{:S(2)}) async-start(s32[64,1,2]{2,1,0:T(1,128)} %bitcast.5), calls=%async_computation.1 | async-start | bytes 65536 | tf_op jit(solution)/shard_map/all_to_all | solution.py:50
  24.7 5.9 collective-permute-start
  43.1 195.7 %all-to-all-start = ((bf16[64,2,64,512]{3,2,1,0:T(8,128)(2,1)}), bf16[64,2,64,512]{3,2,1,0:T(8,128)(2,1)}, u32[]{:S(2)}, u32[]{:S(2)}) async-start(bf16[64,2,64,512]{3,2,1,0:T(8,128)(2,1)} %bitcast.66), calls=%async_computation | async-start | bytes 16777216 | tf_op jit(solution)/shard_map/all_to_all | solution.py:49
  61.3 23.9 %copy-start.2 = (bf16[16,128,512]{2,1,0:T(8,128)(2,1)S(1)}, bf16[16,128,512]{2,1,0:T(8,128)(2,1)}, u32[]{:S(2)}) copy-start(bf16[16,128,512]{2,1,0:T(8,128)(2,1)} %param.8) | copy-start | bytes 6291460
  272.4 30.0 %all-to-all-start.2 = ((bf16[64,2,256]{2,1,0:T(2,128)(2,1)}), bf16[64,2,256]{2,1,0:T(2,128)(2,1)S(1)}, u32[]{:S(2)}, u32[]{:S(2)}) async-start(bf16[64,2,256]{2,1,0:T(2,128)(2,1)} %reshape.242), calls=%async_computation.2 | async-start | bytes 131072 | tf_op jit(solution)/shard_map/all_to_all | solution.py:70
  302.4 208.6 %all-to-all-start.3 = ((bf16[64,2,64,512]{3,2,1,0:T(8,128)(2,1)}), bf16[64,2,64,512]{3,2,1,0:T(8,128)(2,1)}, u32[]{:S(2)}, u32[]{:S(2)}) async-start(bf16[64,2,64,512]{3,2,1,0:T(8,128)(2,1)} %bitcast.67), calls=%async_computation.3 | async-start | bytes 16777216 | tf_op jit(solution)/shard_map/all_to_all | solution.py:69
  312.9 107.3 %all-gather.2.cloned.1.call-start = ((), (), s32[]{:S(2)}) async-start(), calls=%async_computation.6 | async-start | bytes 4259840 | tf_op jit(solution)/shard_map/all_gather | solution.py:84
  511.0 54.3 %all-to-all-start.4 = ((bf16[4,512,1024]{2,1,0:T(8,128)(2,1)}), bf16[4,512,1024]{2,1,0:T(8,128)(2,1)}, u32[]{:S(2)}, u32[]{:S(2)}) async-start(bf16[4,512,1024]{2,1,0:T(8,128)(2,1)} %bitcast.70), calls=%async_computation.4 | async-start | bytes 8388608 | tf_op jit(solution)/shard_map/all_to_all | solution.py:85
  515.9 142.6 %reduce-scatter.2.cloned.1.call-start = ((), (), s32[]{:S(2)}) async-start(), calls=%async_computation.7 | async-start | bytes 10485760 | tf_op jit(solution)/shard_map/reduce_scatter | solution.py:87
  529.5 42.2 %collective-permute-start.1 = (bf16[64,512]{1,0:T(8,128)(2,1)S(1)}, bf16[64,512]{1,0:T(8,128)(2,1)S(1)}, u32[]{:S(2)}, u32[]{:S(2)}) collective-permute-start(bf16[64,512]{1,0:T(8,128)(2,1)S(1)} %bitcast.78), channel_id=1, source_target_pairs={{0,4},{4,8},{8,12},{12,16},{16,20},{20,24},{24,28},{28,32},{32,36}... | collective-permute-start | bytes 196616 | tf_op jit(solution)/shard_map/ppermute | solution.py:15
  571.8 86.7 %copy-start.1 = (bf16[16,128,512]{2,1,0:T(8,128)(2,1)S(1)}, bf16[16,128,512]{2,1,0:T(8,128)(2,1)}, u32[]{:S(2)}) copy-start(bf16[16,128,512]{2,1,0:T(8,128)(2,1)} %param.7) | copy-start | bytes 6291460
Sparse Core Ops, SparseCore 0:
  316.5 103.6 all-gather.1
  581.1 77.3 reduce-scatter.1
where the time goes:
time: 667 us; the launch traced here: 665 us
  waiting for transfers between devices  434 us (65%)
  local copies, waits for them, and re-layouts  106 us (16%)
  starting transfers between devices  48.6 us (7%)
  matrix products  44.8 us (7%)
  other arithmetic  19 us (3%)
  between operations  13.7 us (2%)
    all_to_all x1, waiting for transfers between devices, per_device(): lax.all_to_all(outgoing, 'seq', split_axis=0, concat_axis=0, tiled=True)  122 us
    all_gather x1, waiting for transfers between devices, per_device(): rows_all = lax.all_gather(out_weight, 'seq', axis=0, tiled=True)  107 us
    all_to_all x1, waiting for transfers between devices, per_device(): lax.all_to_all(partial_value, 'seq', split_axis=0, concat_axis=0, tiled=T...  90.8 us
    reduce_scatter x1, waiting for transfers between devices, per_device(): lax.psum_scatter(terms.astype(jnp.bfloat16), 'tp', scatter_dimension=1, t...  77.5 us
    all_to_all x1, waiting for transfers between devices, per_device(): lax.all_to_all(rows_all, 'tp', split_axis=0, concat_axis=1, tiled=True)  33.8 us
    reshape x1, local copies, waits for them, and re-layouts, per_device(): db_keys[asked_rows].reshape(sources, slots_in, NLEN, heads_here, HD)  23.9 us
    reshape x1, local copies, waits for them, and re-layouts, per_device(): db_values[asked_rows].reshape(sources, slots_in, NLEN, heads_here, HD)  23.7 us
    dot_general x1, matrix products, per_device(): jnp.einsum('scqhd,sckhd->schqk', query_heads, key_rows, preferred_element...  19.9 us
  transfers between devices with their start and end apart: 9, of which 6 were waited for; matrix products, arithmetic and copies ran while one was open for 18% of the time, Pallas kernels for 0%

commit v1 on v0

--- a/solution.py
+++ b/solution.py
@@ -81,7 +81,9 @@
     attended = attended.reshape(blocks * BLOCK, feature_cols)
     tail_rows = from_behind(attended[-BLOCK:], "seq", 1)
     placed = jnp.concatenate([tail_rows[1:], attended[: tok_rows - (BLOCK - 1)]], axis=0)
-    rows_all = lax.all_gather(out_weight, "seq", axis=0, tiled=True)
+    rows_all = jnp.concatenate(
+        lax.all_to_all(jnp.stack([out_weight] * lax.axis_size("seq")), "seq", 0, 0), axis=0
+    )
     own_rows = lax.all_to_all(rows_all, "tp", split_axis=0, concat_axis=1, tiled=True)
     terms = jnp.dot(placed, own_rows, preferred_element_type=jnp.float32)
     mixed = lax.psum_scatter(terms.astype(jnp.bfloat16), "tp", scatter_dimension=1, tiled=True)

time: 667 us -> 733 us (1.099)
  blocking collectives: 0 us -> 393 us
  waiting for transfers between devices: 434 us -> 114 us
  starting transfers between devices: 48.6 us -> 38.8 us
    all_to_all x0 -> x2, blocking collectives: none -> 393 us  [the longest x1 197 us: per_device(): lax.all_to_all(partial_value, 'seq', split_axis=0, concat_axis=0, tiled=T...]
    all_to_all x2 -> x1, waiting for transfers between devices: 213 us -> 0.01 us  [per_device(): lax.all_to_all(jnp.stack([out_weight] * lax.axis_size('seq')), 'seq', 0, 0)]
    all_gather x1 -> x0, waiting for transfers between devices: 107 us -> none  [per_device(): rows_all = lax.all_gather(out_weight, 'seq', axis=0, tiled=True)]
    all_to_all x2 -> x1, starting transfers between devices: 20.5 us -> 6.02 us  [per_device(): lax.all_to_all(jnp.stack([out_weight] * lax.axis_size('seq')), 'seq', 0, 0)]
  transfers between devices with their start and end apart: 9 -> 7, of which waited for: 6 -> 3; matrix products, arithmetic and copies ran while one was open for 18% -> 21% of each run, Pallas kernels for 0% -> 0%
where the time goes in v1:
time: 733 us; the launch traced here: 731 us
  blocking collectives  393 us (54%)
  waiting for transfers between devices  114 us (16%)
  local copies, waits for them, and re-layouts  108 us (15%)
  matrix products  44.8 us (6%)
  starting transfers between devices  38.8 us (5%)
  other arithmetic  19 us (3%)
  between operations  13.7 us (2%)
    all_to_all x1, blocking collectives, per_device(): lax.all_to_all(partial_value, 'seq', split_axis=0, concat_axis=0, tiled=T...  197 us
    all_to_all x1, blocking collectives, per_device(): lax.all_to_all(outgoing, 'seq', split_axis=0, concat_axis=0, tiled=True)  196 us
    reduce_scatter x1, waiting for transfers between devices, per_device(): lax.psum_scatter(terms.astype(jnp.bfloat16), 'tp', scatter_dimension=1, t...  78.5 us
    all_to_all x1, waiting for transfers between devices, per_device(): lax.all_to_all(rows_all, 'tp', split_axis=0, concat_axis=1, tiled=True)  32.9 us
    reshape x1, local copies, waits for them, and re-layouts, per_device(): db_keys[asked_rows].reshape(sources, slots_in, NLEN, heads_here, HD)  23.8 us
    reshape x1, local copies, waits for them, and re-layouts, per_device(): db_values[asked_rows].reshape(sources, slots_in, NLEN, heads_here, HD)  23.7 us
    dot_general x1, matrix products, per_device(): jnp.einsum('scqhd,sckhd->schqk', query_heads, key_rows, preferred_element...  19.9 us
    dot_general x1, matrix products, per_device(): jnp.einsum('schqk,sckhd->scqhd', weights, value_rows, preferred_element_t...  15.7 us
  transfers between devices with their start and end apart: 7, of which 3 were waited for; matrix products, arithmetic and copies ran while one was open for 21% of the time, Pallas kernels for 0%

profile of v1, /device:TPU:1, one launch (start us, length us, event | category | flops | bytes accessed | tf_op | source)
XLA Modules:
  0.0 730.7 jit_solution(9906214269806255350)
XLA Ops:
  6.5 0.0 copy-start
  6.5 0.8 broadcast_multiply_fusion
  7.4 0.8 copy.49
  8.1 0.1 copy.48
  8.2 0.1 mul.32
  8.3 0.1 eq.15
  8.4 0.2 convert_reduce_fusion
  8.6 0.8 copy.50
  9.3 0.1 reshape.236
  9.4 0.7 scatter_custom_fusion.1
  10.1 0.7 all_to_all.35
  10.9 13.0 %all-to-all-start.1 = ((s32[64,1,2]{2,1,0:T(1,128)}), s32[64,1,2]{2,1,0:T(1,128)S(1)}, u32[]{:S(2)}, u32[]{:S(2)}) async-start(s32[64,1,2]{2,1,0:T(1,128)} %bitcast.5), calls=%async_computation.1 | async-start | bytes 65536 | tf_op jit(solution)/shard_map/all_to_all | solution.py:50
  23.8 0.8 slice.22
  24.7 2.4 collective-permute-start
  27.1 1.4 slice.21
  28.5 2.0 collective-permute-done
  30.6 0.1 pad_maximum_fusion
  30.6 2.0 gather_fusion
  32.6 4.3 broadcast_in_dim.4
  36.9 6.2 scatter_fusion
  43.1 0.0 all-to-all-done.1
  43.1 0.0 copy-start.3
  43.1 196.2 %all_to_all.51 = bf16[64,2,64,512]{3,2,1,0:T(8,128)(2,1)} all-to-all(bf16[64,2,64,512]{3,2,1,0:T(8,128)(2,1)} %bitcast.66), channel_id=1, replica_groups=mesh['seq'=64,'tp'=4] {'seq'}, dimensions={0} | all-to-all | bytes 16777216 | tf_op jit(solution)/shard_map/all_to_all | solution.py:49
  239.3 0.0 copy-done.3
  239.3 2.5 stack.2
  241.8 6.0 all-to-all-start.4
  247.8 0.1 copy.52
  247.9 0.1 copy.53
  248.0 0.1 reshape.194
  248.1 0.0 copy-done
  248.1 7.8 %gather_fusion.1 = bf16[128,128,512]{2,1,0:T(8,128)(2,1)} fusion(bf16[16,128,512]{2,1,0:T(8,128)(2,1)S(1)} %copy-done, s32[1024]{0:T(1024)S(1)} %pad_clamp_fusion.1), kind=kCustom, calls=%fused_computation.1 | custom fusion | bytes 33554944 | tf_op jit(solution)/shard_map/gather | solution.py:53
  255.9 23.8 %reshape.174 = bf16[64,2,128,4,128]{4,3,2,1,0:T(4,128)(2,1)} reshape(bf16[128,128,512]{2,1,0:T(8,128)(2,1)} %gather_fusion.1) | data formatting | bytes 33554432 | tf_op jit(solution)/shard_map/reshape | solution.py:53
  279.8 0.0 copy-done.2
  279.8 7.9 %gather_fusion.3 = bf16[128,128,512]{2,1,0:T(8,128)(2,1)} fusion(bf16[16,128,512]{2,1,0:T(8,128)(2,1)S(1)} %copy-done.2, s32[1024]{0:T(1024)S(1)} %pad_clamp_fusion.1), kind=kCustom, calls=%fused_computation.3 | custom fusion | bytes 33554944 | tf_op jit(solution)/shard_map/gather | solution.py:54
  287.7 23.7 %reshape.178 = bf16[64,2,128,4,128]{4,3,2,1,0:T(4,128)(2,1)} reshape(bf16[128,128,512]{2,1,0:T(8,128)(2,1)} %gather_fusion.3) | data formatting | bytes 33554432 | tf_op jit(solution)/shard_map/reshape | solution.py:54
  311.4 19.9 %multiply_reduce_fusion = (f32[64,2,4,64]{3,2,1,0:T(4,128)S(1)}, f32[64,2,4,64,128]{4,3,2,1,0:T(8,128)}) fusion(bf16[64,2,128,4,128]{4,3,2,1,0:T(4,128)(2,1)} %reshape.174, bf16[64,2,64,512]{3,2,1,0:T(8,128)(2,1)} %all_to_all.51), kind=kOutput, calls=%fused_computation.13 | convolution fusion | flops 1082097664 | bytes 42074112 | tf_op jit(solution)/shard_map/scqhd,sckhd->schqk/dot_general | solution.py:57
  331.3 12.6 %exponential_reduce_fusion = f32[64,2,4,64]{3,2,1,0:T(4,128)S(1)} fusion(f32[64,2,4,64,128]{4,3,2,1,0:T(8,128)} %get-tuple-element.8, f32[64,2,4,64]{3,2,1,0:T(4,128)S(1)} %get-tuple-element.7), kind=kLoop, calls=%fused_computation.12 | loop fusion | flops 12550144 | bytes 17039360 | tf_op jit(solution)/shard_map/reduce_sum | solution.py:61
  343.9 0.1 fusion.24
  344.1 0.8 reshape.246
  344.9 0.0 all-to-all-done.4
  344.9 10.4 %all-to-all-start.2 = ((bf16[64,2,256]{2,1,0:T(2,128)(2,1)}), bf16[64,2,256]{2,1,0:T(2,128)(2,1)S(1)}, u32[]{:S(2)}, u32[]{:S(2)}) async-start(bf16[64,2,256]{2,1,0:T(2,128)(2,1)} %reshape.246), calls=%async_computation.2 | async-start | bytes 131072 | tf_op jit(solution)/shard_map/all_to_all | solution.py:70
  355.3 15.7 %convert_bitcast_fusion = bf16[64,2,4,8,8,128]{5,4,3,2,1,0:T(8,128)(2,1)} fusion(bf16[64,2,128,4,128]{4,3,2,1,0:T(4,128)(2,1)} %reshape.178, f32[64,2,4,64,128]{4,3,2,1,0:T(8,128)} %get-tuple-element.8, f32[64,2,4,64]{3,2,1,0:T(4,128)S(1)} %get-tuple-element.6), kind=kOutput, calls=%fused_computation.17 | convolution fusion | flops 1090519040 | bytes 42074112 | tf_op jit(solution)/shard_map/schqk,sckhd->scqhd/dot_general | solution.py:63
  371.0 8.4 %copy.81 = bf16[64,2,4,8,8,128]{5,4,2,3,1,0:T(8,128)(2,1)} copy(bf16[64,2,4,8,8,128]{5,4,3,2,1,0:T(8,128)(2,1)} %convert_bitcast_fusion) | data formatting | bytes 16777216 | tf_op jit(solution)/shard_map/reshape | solution.py:66
  379.4 0.0 all-to-all-done.2
  379.4 196.7 %all_to_all.52 = bf16[64,2,64,512]{3,2,1,0:T(8,128)(2,1)} all-to-all(bf16[64,2,64,512]{3,2,1,0:T(8,128)(2,1)} %bitcast.67), channel_id=1, replica_groups=mesh['seq'=64,'tp'=4] {'seq'}, dimensions={0} | all-to-all | bytes 16777216 | tf_op jit(solution)/shard_map/all_to_all | solution.py:69
  576.1 4.9 all-to-all-start.5
  581.0 0.0 reduce-scatter.2.cloned.1.call-start
  581.1 0.1 reshape.247
  581.3 0.6 gather_fusion.2
  582.0 0.4 copy.56
  582.4 4.1 gather_fusion.4
  586.5 3.0 reshape.183
  589.5 5.0 multiply_reduce_fusion.1
  594.5 2.1 collective-permute-start.1
  596.6 32.9 %all-to-all-done.5 = bf16[4,512,1024]{2,1,0:T(8,128)(2,1)} async-done(((bf16[4,512,1024]{2,1,0:T(8,128)(2,1)}), bf16[4,512,1024]{2,1,0:T(8,128)(2,1)}, u32[]{:S(2)}, u32[]{:S(2)}) %all-to-all-start.5) | async-done | bytes 4194336 | tf_op jit(solution)/shard_map/all_to_all | solution.py:87
  629.6 6.2 copy.59
  635.8 0.2 copy.82
  636.0 0.1 slice.41
  636.1 0.0 collective-permute-done.1
  636.1 0.0 copy-start.1
  636.1 9.2 %convolution_convert_fusion = bf16[1024,4096]{1,0:T(8,128)(2,1)} fusion(bf16[512,4096]{0,1:T(8,128)(2,1)} %bitcast.71, bf16[961,512]{1,0:T(8,128)(2,1)S(1)} %slice.41, bf16[63,512]{1,0:T(8,128)(2,1)S(1)} %slice.40), kind=kOutput, calls=%fused_computation.20 | convolution fusion | flops 4301258752 | bytes 13631488 | tf_op jit(solution)/shard_map/dot_general | solution.py:88
  645.3 0.0 reduce-scatter.2.cloned.1.call-update
  645.3 78.5 %reduce-scatter.2.cloned.1.call-done = bf16[1024,1024]{1,0:T(8,128)(2,1)} async-done(((bf16[1024,4096]{1,0:T(8,128)(2,1)}), bf16[1024,1024]{1,0:T(8,128)(2,1)}) %reduce-scatter.2.cloned.1.call-update) | async-done | bytes 2097168 | tf_op jit(solution)/shard_map/reduce_scatter | solution.py:89
  723.8 0.0 copy-done.1
  (15 shorter events, 0.2 us)
Async XLA Ops:
  6.5 241.6 %copy-start = (bf16[16,128,512]{2,1,0:T(8,128)(2,1)S(1)}, bf16[16,128,512]{2,1,0:T(8,128)(2,1)}, u32[]{:S(2)}) copy-start(bf16[16,128,512]{2,1,0:T(8,128)(2,1)} %param.7) | copy-start | bytes 6291460
  10.9 32.3 %all-to-all-start.1 = ((s32[64,1,2]{2,1,0:T(1,128)}), s32[64,1,2]{2,1,0:T(1,128)S(1)}, u32[]{:S(2)}, u32[]{:S(2)}) async-start(s32[64,1,2]{2,1,0:T(1,128)} %bitcast.5), calls=%async_computation.1 | async-start | bytes 65536 | tf_op jit(solution)/shard_map/all_to_all | solution.py:50
  24.7 5.9 collective-permute-start
  43.1 196.2 %copy-start.3 = (bf16[32,1024]{1,0:T(8,128)(2,1)S(1)}, bf16[32,1024]{1,0:T(8,128)(2,1)}, u32[]{:S(2)}) copy-start(bf16[32,1024]{1,0:T(8,128)(2,1)} %param.11) | copy-start | bytes 196612
  241.8 103.1 %all-to-all-start.4 = ((bf16[64,32,1024]{2,1,0:T(8,128)(2,1)}), bf16[64,32,1024]{2,1,0:T(8,128)(2,1)}, u32[]{:S(2)}, u32[]{:S(2)}) async-start(bf16[64,32,1024]{2,1,0:T(8,128)(2,1)} %stack.2), calls=%async_computation.4 | async-start | bytes 8388608 | tf_op jit(solution)/shard_map/all_to_all | solution.py:85
  255.9 23.8 %copy-start.2 = (bf16[16,128,512]{2,1,0:T(8,128)(2,1)S(1)}, bf16[16,128,512]{2,1,0:T(8,128)(2,1)}, u32[]{:S(2)}) copy-start(bf16[16,128,512]{2,1,0:T(8,128)(2,1)} %param.8) | copy-start | bytes 6291460
  344.9 34.6 %all-to-all-start.2 = ((bf16[64,2,256]{2,1,0:T(2,128)(2,1)}), bf16[64,2,256]{2,1,0:T(2,128)(2,1)S(1)}, u32[]{:S(2)}, u32[]{:S(2)}) async-start(bf16[64,2,256]{2,1,0:T(2,128)(2,1)} %reshape.246), calls=%async_computation.2 | async-start | bytes 131072 | tf_op jit(solution)/shard_map/all_to_all | solution.py:70
  576.1 53.4 %all-to-all-start.5 = ((bf16[4,512,1024]{2,1,0:T(8,128)(2,1)}), bf16[4,512,1024]{2,1,0:T(8,128)(2,1)}, u32[]{:S(2)}, u32[]{:S(2)}) async-start(bf16[4,512,1024]{2,1,0:T(8,128)(2,1)} %bitcast.12), calls=%async_computation.5 | async-start | bytes 8388608 | tf_op jit(solution)/shard_map/all_to_all | solution.py:87
  581.0 142.8 %reduce-scatter.2.cloned.1.call-start = ((), (), s32[]{:S(2)}) async-start(), calls=%async_computation.7 | async-start | bytes 10485760 | tf_op jit(solution)/shard_map/reduce_scatter | solution.py:89
  594.5 41.5 %collective-permute-start.1 = (bf16[64,512]{1,0:T(8,128)(2,1)S(1)}, bf16[64,512]{1,0:T(8,128)(2,1)S(1)}, u32[]{:S(2)}, u32[]{:S(2)}) collective-permute-start(bf16[64,512]{1,0:T(8,128)(2,1)S(1)} %bitcast.78), channel_id=1, source_target_pairs={{0,4},{4,8},{8,12},{12,16},{16,20},{20,24},{24,28},{28,32},{32,36}... | collective-permute-start | bytes 196616 | tf_op jit(solution)/shard_map/ppermute | solution.py:15
  636.1 87.8 %copy-start.1 = (bf16[16,128,512]{2,1,0:T(8,128)(2,1)S(1)}, bf16[16,128,512]{2,1,0:T(8,128)(2,1)}, u32[]{:S(2)}) copy-start(bf16[16,128,512]{2,1,0:T(8,128)(2,1)} %param.7) | copy-start | bytes 6291460
Sparse Core Ops, SparseCore 0:
  645.4 78.3 reduce-scatter.1
